TPU v7x, 768 devices: a whole 4x8x12 slice. The times are simulated.
768 devices in a mesh: space: 64 (over y, x, core), tm: 12 (over z).
Axes of the slice: x: 4, y: 8, z: 12, core: 2. Of those that a mesh axis runs over, the one named last changes fastest.
Arguments:
- velocity: bfloat16 [3, 24576, 3072], P(None, 'space', 'tm'), may hold values from -16 to 16
- metric: float32 [24576], P('space'), may hold values from 0.5 to 2
Outputs:
- tiles: float32 [3072, 3072], P('tm', 'space')
All inputs are finite; a program needn't handle non-finite values.
Results may differ from a plain program's by a relative error of at most 0.0016.
Values may be sent and summed in bfloat16 or wider, within the bound.
A program may use at most 32 MiB of HBM per device.

v0:
```python
import jax
import jax.numpy as jnp
from jax import lax
from jax.sharding import PartitionSpec as P


def padded_2(cells, sides, width):
    for axis, dim in sides:
        count = lax.axis_size(axis)
        ends = count - 1
        head = lax.slice_in_dim(cells, 0, width, axis=dim)
        tail = lax.slice_in_dim(cells, cells.shape[dim] - width, cells.shape[dim], axis=dim)
        cells = jnp.concatenate(
            [
                lax.ppermute(tail, axis, [(i, (i + 1) % count) for i in range(ends)]),
                cells,
                lax.ppermute(head, axis, [((i + 1) % count, i) for i in range(ends)]),
            ],
            axis=dim,
        )
    return cells


def from_behind(value, axis, steps):
    count = lax.axis_size(axis)
    pairs = [(source, (source + steps) % count) for source in range(count)]
    return lax.ppermute(value, axis, pairs)


def cross_product(left, right):
    return lax.dot_general(
        left, right, (((0,), (0,)), ((), ())), preferred_element_type=jnp.float32
    )


def body(velocity, metric):
    padded = padded_2(velocity, (("space", 1),), 1)
    field = padded.astype(jnp.float32)
    center = field[:, 1:-1]
    gradient = metric[None, :, None] * (field[:, 2:] - field[:, :-2]) * 0.5
    helical = gradient[2] + center[0] * gradient[1] - center[1] * gradient[0]
    snapshot_panel = jnp.stack([gradient[0], gradient[1], helical]).astype(jnp.bfloat16)
    snapshot_panel = snapshot_panel.reshape(3 * velocity.shape[1], velocity.shape[2])
    gram_matrix = lax.psum(cross_product(snapshot_panel, snapshot_panel), "space")
    following = from_behind(snapshot_panel[:, :1], "tm", -1)
    shifted = jnp.concatenate([snapshot_panel[:, 1:], following], axis=1)
    partial_value = cross_product(snapshot_panel, lax.all_gather(shifted, "tm", axis=1, tiled=True))
    summed = lax.psum_scatter(partial_value, "space", scatter_dimension=1, tiled=True)
    factor = jnp.linalg.cholesky(gram_matrix)
    return lax.linalg.triangular_solve(factor, summed, left_side=True, lower=True)


def solution(mesh):
    in_specs = (P(None, "space", "tm"), P("space"))
    out_specs = P("tm", "space")
    return jax.shard_map(body, mesh=mesh, in_specs=in_specs, out_specs=out_specs, check_vma=False)
```

profile of v0, /device:TPU:2, one launch (start us, length us, event | category | flops | bytes accessed | tf_op | source)
XLA Modules:
  0.0 412.1 jit_solution(6040998906770936011)
XLA Ops:
  7.4 0.7 fusion.13
  8.1 1.9 collective-permute-start
  10.0 3.6 collective-permute-start.1
  13.7 1.3 collective-permute-done.1
  15.0 1.2 maximum_convert_fusion.1
  16.4 0.2 fusion.2
  16.8 14.6 %collective-permute-start.2 = (bf16[1152,1]{1,0:T(8,128)(2,1)S(1)}, bf16[1152,1]{1,0:T(8,128)(2,1)S(1)}, u32[]{:S(2)}, u32[]{:S(2)}) collective-permute-start(bf16[1152,1]{1,0:T(8,128)(2,1)S(1)} %slice.115), channel_id=1, source_target_pairs={{0,11},{1,0},{2,1},{3,2},{4,3},{5,4},{6,5},{7,6},{8,7},{9,8},{10,9... | collective-permute-start | bytes 6920 | tf_op jit(solution)/shard_map/ppermute | solution.py:27
  31.3 0.3 slice.114
  31.6 6.6 %collective-permute-done.2 = bf16[1152,1]{1,0:T(8,128)(2,1)S(1)} collective-permute-done((bf16[1152,1]{1,0:T(8,128)(2,1)S(1)}, bf16[1152,1]{1,0:T(8,128)(2,1)S(1)}, u32[]{:S(2)}, u32[]{:S(2)}) %collective-permute-start.2) | collective-permute-done | bytes 2336 | tf_op jit(solution)/shard_map/ppermute | solution.py:27
  38.2 1.0 pad_maximum_fusion
  39.3 1.1 convolution_bitcast_fusion
  40.5 105.4 %all-gather.2.cloned.1.call-done = bf16[1152,3072]{1,0:T(8,128)(2,1)} async-done(((bf16[1152,256]{1,0:T(8,128)(2,1)}), bf16[1152,3072]{1,0:T(8,128)(2,1)}) %all-gather.2.cloned.1.call-update) | async-done | bytes 7077904 | tf_op jit(solution)/shard_map/all_gather | solution.py:47
  145.8 7.7 %fusion.14 = f32[256,3072]{0,1:T(8,128)} fusion(bf16[1152,256]{1,0:T(8,128)(2,1)S(1)} %bitcast.40, bf16[1152,3072]{1,0:T(8,128)(2,1)} %all-gather.2.cloned.1.call-done), kind=kOutput, calls=%fused_computation.41 | convolution fusion | flops 1811939328 | bytes 10813440 | tf_op jit(solution)/shard_map/dot_general | solution.py:31
  153.5 85.3 %all-reduce.3.cloned.1.call-done = f32[256,256]{0,1:T(8,128)} async-done(((f32[256,256]{0,1:T(8,128)}), f32[256,256]{0,1:T(8,128)}) %all-reduce.3.cloned.1.call-update) | async-done | bytes 262160 | tf_op jit(solution)/shard_map/psum | solution.py:44
  238.8 1.1 copy.5
  239.9 1.0 fusion.4
  240.9 11.7 %cholesky.50 = f32[128,128]{1,0:T(8,128)S(1)} custom-call(f32[128,128]{1,0:T(8,128)S(1)} %cholesky.118), custom_call_target="Cholesky" | custom-call | tf_op jit(solution)/shard_map/jit(cholesky)/cholesky | solution.py:49
  252.7 9.8 %custom-call.14 = f32[1,128,128]{1,2,0:T(8,128)S(1)} custom-call(f32[1,128,128]{2,1,0:T(8,128)S(1)} %get-tuple-element.28), custom_call_target="InvertDiagBlocksLowerTriangular" | custom-call | tf_op jit(solution)/shard_map/jit(cholesky)/cholesky | solution.py:49
  262.5 0.2 constant_dynamic-update-slice_fusion.1
  262.7 0.3 convolution_subtract_fusion
  263.0 11.9 %cholesky.105 = f32[128,128]{1,0:T(8,128)S(1)} custom-call(f32[128,128]{1,0:T(8,128)S(1)} %convolution_subtract_fusion), custom_call_target="Cholesky" | custom-call | tf_op jit(solution)/shard_map/jit(cholesky)/cholesky | solution.py:49
  274.9 0.7 compare_reduce_fusion
  277.0 3.9 while.1
  277.0 0.6 fusion.24
  277.6 1.3 bitcast_dynamic-update-slice_fusion.2
  279.0 0.6 fusion.24
  279.6 1.3 bitcast_dynamic-update-slice_fusion.2
  280.9 19.7 %custom-call.15 = f32[2,128,128]{1,2,0:T(8,128)S(1)} custom-call(f32[2,128,128]{2,1,0:T(8,128)S(1)} %get-tuple-element.12), custom_call_target="InvertDiagBlocksLowerTriangular" | custom-call | tf_op jit(solution)/shard_map/triangular_solve | solution.py:50
  300.6 101.4 %reduce-scatter.2.cloned.1.call-done = f32[256,48]{0,1:T(8,128)} async-done(((f32[256,3072]{0,1:T(8,128)}), f32[256,48]{0,1:T(8,128)}) %reduce-scatter.2.cloned.1.call-update) | async-done | bytes 49168 | tf_op jit(solution)/shard_map/reduce_scatter | solution.py:48
  402.0 0.9 fusion.7
  402.9 1.0 convolution_subtract_fusion.1
  404.0 0.6 pad_maximum_fusion.1
  (24 shorter events, 0.9 us)
Async XLA Ops:
  7.4 8.8 %copy-start = (f32[384]{0:T(512)S(1)}, f32[384]{0:T(512)}, u32[]{:S(2)}) copy-start(f32[384]{0:T(512)} %param.3) | copy-start | bytes 4612
  7.4 138.4 %all-gather.2.cloned.1.call-start = ((), (), s32[]{:S(2)}) async-start(), calls=%async_computation.2 | async-start | bytes 7667712 | tf_op jit(solution)/shard_map/all_gather | solution.py:47
  8.1 5.6 %collective-permute-start = (bf16[3,1,256]{2,1,0:T(2,128)(2,1)S(1)}, bf16[3,1,256]{2,1,0:T(2,128)(2,1)S(1)}, u32[]{:S(2)}, u32[]{:S(2)}) collective-permute-start(bf16[3,1,256]{2,1,0:T(2,128)(2,1)S(1)} %get-tuple-element.23), channel_id=1, source_target_pairs={{0,12},{12,24},{24,36},{36,48},{48,60},{60,72},{72,84},{84,96},{96... | collective-permute-start | bytes 4616 | tf_op jit(solution)/shard_map/ppermute | solution.py:15
  10.0 4.9 %collective-permute-start.1 = (bf16[3,1,256]{2,1,0:T(2,128)(2,1)S(1)}, bf16[3,1,256]{2,1,0:T(2,128)(2,1)S(1)}, u32[]{:S(2)}, u32[]{:S(2)}) collective-permute-start(bf16[3,1,256]{2,1,0:T(2,128)(2,1)S(1)} %get-tuple-element.24), channel_id=1, source_target_pairs={{12,0},{24,12},{36,24},{48,36},{60,48},{72,60},{84,72},{96,84},{10... | collective-permute-start | bytes 4616 | tf_op jit(solution)/shard_map/ppermute | solution.py:17
  16.8 21.4 %collective-permute-start.2 = (bf16[1152,1]{1,0:T(8,128)(2,1)S(1)}, bf16[1152,1]{1,0:T(8,128)(2,1)S(1)}, u32[]{:S(2)}, u32[]{:S(2)}) collective-permute-start(bf16[1152,1]{1,0:T(8,128)(2,1)S(1)} %slice.115), channel_id=1, source_target_pairs={{0,11},{1,0},{2,1},{3,2},{4,3},{5,4},{6,5},{7,6},{8,7},{9,8},{10,9... | collective-permute-start | bytes 6920 | tf_op jit(solution)/shard_map/ppermute | solution.py:27
  39.2 199.6 %all-reduce.3.cloned.1.call-start = ((), (), s32[]{:S(2)}) async-start(), calls=%async_computation.1 | async-start | bytes 524288 | tf_op jit(solution)/shard_map/psum | solution.py:44
  40.4 361.6 %reduce-scatter.2.cloned.1.call-start = ((), (), s32[]{:S(2)}) async-start(), calls=%async_computation.3 | async-start | bytes 3194880 | tf_op jit(solution)/shard_map/reduce_scatter | solution.py:48
Sparse Core Ops, SparseCore 0:
  39.3 106.4 all-gather.1
Sparse Core Ops, SparseCore 1:
  43.2 195.6 all-reduce.2
  244.8 157.1 reduce-scatter.1
where the time goes:
time: 413 us; the launch traced here: 412 us
  waiting for transfers between devices  300 us (73%)
  other arithmetic  58.2 us (14%)
  starting transfers between devices  20.2 us (5%)
  between operations  16.3 us (4%)
  matrix products  11.3 us (3%)
  local copies, waits for them, and re-layouts  6.11 us (1%)
    all_gather x1, waiting for transfers between devices, body(): lax.all_gather(shifted, 'tm', axis=1, tiled=True)  105 us
    reduce_scatter x1, waiting for transfers between devices, body(): lax.psum_scatter(partial_value, 'space', scatter_dimension=1, tiled=True)  101 us
    psum x1, waiting for transfers between devices, body(): lax.psum(cross_product(snapshot_panel, snapshot_panel), 'space')  85.3 us
    another operation x6, other arithmetic, body(): factor = jnp.linalg.cholesky(gram_matrix)  34.2 us
    another operation x4, other arithmetic, body(): lax.linalg.triangular_solve(factor, summed, left_side=True, lower=True)  20.3 us
    ppermute x1, starting transfers between devices, from_behind(): return lax.ppermute(value, axis, pairs)  14.6 us
    dot_general x2, matrix products, cross_product(): lax.dot_general(left, right, (((0,), (0,)), ((), ())), preferred_element_...  8.79 us
  transfers between devices with their start and end apart: 6, of which 5 were waited for; matrix products, arithmetic and copies ran while one was open for 17% of the time, Pallas kernels for 0%

commit v1 on v0

v1 whole, which is shorter than its diff:
```python
import jax
import jax.numpy as jnp
from jax import lax
from jax.experimental import pallas as pl
from jax.experimental.pallas import tpu as pltpu
from jax.sharding import PartitionSpec as P

MESH = pl.DeviceIdType.MESH
X, Y, Z = 4, 8, 12
SPACE = 2 * X * Y
S = 256
PAIRS = ((0, 0), (0, 1), (-1, 1), (-1, 2), (-2, 2), (-2, 3), (-3, 3))
LAST = len(PAIRS) - 1
REACH = 3
BLOCK = 32
NT = (((1,), (1,)), ((), ()))
NN = (((1,), (0,)), ((), ()))
F32 = jnp.float32


def exact_dot(left, right, dims):
    return lax.dot_general(
        left, right, dims, precision=lax.Precision.HIGHEST, preferred_element_type=F32
    )


def factor_step(table, j):
    low = j * BLOCK
    rows = table[low : low + BLOCK, :]
    row_at = lax.broadcasted_iota(jnp.int32, (BLOCK, BLOCK), 0)
    lane_at = lax.broadcasted_iota(jnp.int32, (BLOCK, BLOCK), 1)
    eye = jnp.where(row_at == lane_at, 1.0, 0.0).astype(F32)
    work = jnp.concatenate([rows[:, low : low + BLOCK], eye], axis=1)
    below = lax.broadcasted_iota(jnp.int32, work.shape, 0)
    for k in range(BLOCK - 1):
        column = jnp.broadcast_to(work[:, k : k + 1], work.shape)
        pivot = jnp.broadcast_to(column[k : k + 1, :], work.shape)
        pivot_row = jnp.broadcast_to(work[k : k + 1, :], work.shape)
        scale = jnp.where(below > k, column / pivot, 0.0)
        work = work - scale * pivot_row
    pivots = jnp.sum(jnp.where(row_at == lane_at, work[:, :BLOCK], 0.0), axis=1, keepdims=True)
    inverse = work[:, BLOCK:] / jnp.sqrt(pivots)
    solved = exact_dot(inverse, rows, NN)
    table[low : low + BLOCK, :] = solved
    if low + BLOCK < S:
        panel = jnp.transpose(solved[:, :S])[low + BLOCK :, :]
        table[low + BLOCK :, :] = table[low + BLOCK :, :] - exact_dot(panel, solved, NN)


def kernel(
    v_ref, m_ref, out_ref,
    xt, halo, part, cr, cs, xr, xs, yr, ys, gram, table, fin,
    halo_send, halo_recv, z_send, z_recv, c_send, c_recv, x_send, x_recv, y_send, y_recv,
    g_send, g_recv, f_send, f_recv,
):
    s = lax.axis_index("space")
    c = lax.axis_index("tm")
    core = lax.rem(s, 2)
    x = lax.rem(lax.div(s, 2), X)
    y = lax.div(s, 2 * X)
    plus, minus = lax.rem(c + 1, Z), lax.rem(c + Z - 1, Z)
    cells = v_ref.shape[1]

    def at(y_at, x_at, core_at):
        return (y_at * X + x_at) * 2 + core_at

    partner = at(y, x, 1 - core)
    x_peers = [at(y, lax.rem(x + t, X), core) for t in range(1, X)]
    y_peers = [at(lax.rem(y + t, Y), x, core) for t in range(1, Y)]

    barrier = pltpu.get_barrier_semaphore()
    greeted = [(lax.rem(s + 1, SPACE), c), (lax.rem(s + SPACE - 1, SPACE), c), (partner, c), (s, plus), (s, minus)]
    greeted += [(peer, c) for peer in x_peers + y_peers]
    for device in greeted:
        pl.semaphore_signal(barrier, inc=1, device_id=device, device_id_type=MESH)
    pl.semaphore_wait(barrier, len(greeted))

    def remote(src, dst, send, recv, device):
        return pltpu.make_async_remote_copy(
            src_ref=src, dst_ref=dst, send_sem=send, recv_sem=recv, device_id=device, device_id_type=MESH
        )

    def arrived(ref, sem):
        pltpu.make_async_copy(ref, ref, sem).wait()

    to_right = remote(v_ref.at[:, cells - 16 :, :], halo.at[0], halo_send.at[0], halo_recv.at[0], (lax.rem(s + 1, SPACE), c))
    to_left = remote(v_ref.at[:, :16, :], halo.at[1], halo_send.at[1], halo_recv.at[1], (lax.rem(s + SPACE - 1, SPACE), c))

    @pl.when(s < SPACE - 1)
    def _():
        to_right.start()

    @pl.when(s > 0)
    def _():
        to_left.start()
        to_right.wait_recv()

    @pl.when(s == 0)
    def _():
        halo[0] = jnp.zeros_like(halo[0])

    @pl.when(s < SPACE - 1)
    def _():
        to_left.wait_recv()

    @pl.when(s == SPACE - 1)
    def _():
        halo[1] = jnp.zeros_like(halo[1])

    row = lax.broadcasted_iota(jnp.int32, (cells, S), 0)
    spacing = jnp.transpose(jnp.broadcast_to(m_ref[...].reshape(1, cells), (128, cells)))
    spacing = jnp.concatenate([spacing, spacing], axis=1)

    def gradient(k):
        field = v_ref[k].astype(F32)
        first = jnp.broadcast_to(halo[0, k].astype(F32)[15:16, :], (cells, S))
        last = jnp.broadcast_to(halo[1, k].astype(F32)[0:1, :], (cells, S))
        after = jnp.where(row == cells - 1, last, pltpu.roll(field, cells - 1, 0))
        before = jnp.where(row == 0, first, pltpu.roll(field, 1, 0))
        return spacing * (after - before) * 0.5

    def hop(t, comp):
        for way, device, sign in ((0, plus, -1), (1, minus, 1)):
            remote(
                xt.at[REACH + sign * (t - 1), comp], xt.at[REACH + sign * t, comp],
                z_send.at[way], z_recv.at[way, t - 1, comp], (s, device),
            ).start()

    def landed(t, comp):
        for way, sign in ((0, -1), (1, 1)):
            arrived(xt.at[REACH + sign * t, comp], z_recv.at[way, t - 1, comp])

    g0 = gradient(0)
    xt[REACH, 0] = jnp.transpose(g0).astype(jnp.bfloat16)
    hop(1, 0)
    g1 = gradient(1)
    xt[REACH, 1] = jnp.transpose(g1).astype(jnp.bfloat16)
    hop(1, 1)
    g2 = gradient(2) + v_ref[0].astype(F32) * g1 - v_ref[1].astype(F32) * g0
    xt[REACH, 2] = jnp.transpose(g2).astype(jnp.bfloat16)
    hop(1, 2)

    def multiply(p, comps):
        low, high = PAIRS[p]
        for comp in comps:
            lower, upper = xt[REACH + low, comp], xt[REACH + high, comp]
            for side, (left, right) in enumerate(((upper, lower), (lower, upper))):
                if side == 1 and p in (0, LAST):
                    continue
                term = lax.dot_general(left, right, NT, preferred_element_type=F32)
                if comp == 0:
                    part[p, side] = term
                else:
                    part[p, side] = part[p, side] + term

    def on_pair(p, body):
        if p == LAST:
            pl.when(core == 0)(body)
        else:
            body()

    def core_copy(p):
        src = part.at[p, 0] if p in (0, LAST) else part.at[p, 1 - core]
        return remote(src, cr.at[p], c_send.at[p], c_recv.at[p], (partner, c))

    def core_start(p):
        if p == LAST:
            pl.when(core == 1)(lambda: core_copy(p).start())
        else:
            core_copy(p).start()

    def x_start(p):
        def body():
            core_copy(p).wait_recv()
            own = part[p, 0] if p in (0, LAST) else part[p, core]
            cs[p] = own + cr[p]
            for t in range(1, X):
                chunk = pl.ds(pl.multiple_of(lax.rem(x + t, X) * 64, 64), 64)
                remote(cs.at[p, chunk], xr.at[p, t - 1], x_send.at[p], x_recv.at[p], (x_peers[t - 1], c)).start()

        on_pair(p, body)

    def y_start(p):
        def body():
            arrived(xr.at[p], x_recv.at[p])
            xs[p] = cs[p, pl.ds(pl.multiple_of(x * 64, 64), 64)] + xr[p, 0] + xr[p, 1] + xr[p, 2]
            for t in range(1, Y):
                chunk = pl.ds(pl.multiple_of(lax.rem(y + t, Y) * 8, 8), 8)
                remote(xs.at[p, chunk], yr.at[p, t - 1], y_send.at[p], y_recv.at[p], (y_peers[t - 1], c)).start()

        on_pair(p, body)

    def y_finish(p):
        arrived(yr.at[p], y_recv.at[p])
        total = xs[p, pl.ds(pl.multiple_of(y * 8, 8), 8)]
        for t in range(Y - 1):
            total = total + yr[p, t]
        return total

    def gram_y():
        rows = pl.ds(pl.multiple_of(x * 64 + y * 8, 8), 8)
        gram[rows] = y_finish(0)
        for t in range(1, Y):
            remote(gram.at[rows], gram.at[rows], g_send.at[0], g_recv.at[0], (y_peers[t - 1], c)).start()

    def gram_x():
        arrived(yr.at[0], g_recv.at[0])
        rows = pl.ds(pl.multiple_of(x * 64, 64), 64)
        for t in range(1, X):
            remote(gram.at[rows], gram.at[rows], g_send.at[1], g_recv.at[1], (x_peers[t - 1], c)).start()

    def gram_finish():
        arrived(xr.at[0], g_recv.at[1])

    unit = x * Y + y

    def place(p):
        low, high = PAIRS[p]
        lanes_of = jnp.where(core == 0, low, high)
        rows_of = jnp.where(core == 0, high, low)
        group = lax.rem(c + lanes_of + Z, Z)
        number = lax.rem(c + rows_of + Z, Z) * 32 + unit
        owner, slot = lax.div(number, 6), lax.rem(number, 6)
        return group, owner, slot

    def to_owner(p):
        group, owner, slot = place(p)
        rows = pl.ds(pl.multiple_of(slot * 8, 8), 8)
        mine = jnp.logical_and(owner == s, group == c)
        return mine, rows, remote(ys.at[p], fin.at[rows], f_send.at[p, 0], f_recv.at[slot], (owner, group))

    def to_ahead(p):
        group, owner, slot = place(p)
        ahead = lax.rem(owner + SPACE - 1, SPACE)
        mine = jnp.logical_and(ahead == s, group == c)
        return slot == 0, mine, remote(ys.at[p], fin.at[48:56], f_send.at[p, 1], f_recv.at[6], (ahead, group))

    def deliver(p):
        def body():
            ys[p] = y_finish(p)
            mine, rows, copy = to_owner(p)

            @pl.when(mine)
            def _():
                fin[rows] = ys[p]

            @pl.when(jnp.logical_not(mine))
            def _():
                copy.start()

            first, mine_ahead, copy_ahead = to_ahead(p)

            @pl.when(jnp.logical_and(first, mine_ahead))
            def _():
                fin[48:56] = ys[p]

            @pl.when(jnp.logical_and(first, jnp.logical_not(mine_ahead)))
            def _():
                copy_ahead.start()

        on_pair(p, body)

    def sent(p):
        def body():
            mine, _, copy = to_owner(p)

            @pl.when(jnp.logical_not(mine))
            def _():
                copy.wait_send()

            first, mine_ahead, copy_ahead = to_ahead(p)

            @pl.when(jnp.logical_and(first, jnp.logical_not(mine_ahead)))
            def _():
                copy_ahead.wait_send()

        on_pair(p, body)

    def collect(slot):
        number = lax.rem(s * 6 + slot, SPACE * 6)
        apart = lax.rem(lax.div(number, 32) - c + Z, Z)
        within = lax.rem(number, 32)
        near = apart <= Z // 2
        home = jnp.where(near, lax.div(apart, 2), Z - lax.div(Z - apart + 1, 2))
        source = at(lax.rem(within, Y), lax.div(within, Y), jnp.where(near, 0, 1))
        own = jnp.logical_and(source == s, lax.rem(home, Z) == 0)
        rows = slice(slot * 8, slot * 8 + 8)

        @pl.when(apart == 0)
        def _():
            fin[rows] = gram[pl.ds(pl.multiple_of(within * 8, 8), 8)]

        @pl.when(jnp.logical_and(apart != 0, jnp.logical_not(own)))
        def _():
            arrived(fin.at[rows], f_recv.at[slot])

    everything = range(3)
    multiply(0, everything)
    core_start(0)
    x_start(0)
    landed(1, 0)
    hop(2, 0)
    y_start(0)
    gram_y()
    gram_x()
    landed(1, 1)
    hop(2, 1)
    gram_finish()
    table[:, :S] = gram[...]
    square = (S, S)
    table[:, S:] = jnp.where(
        lax.broadcasted_iota(jnp.int32, square, 0) == lax.broadcasted_iota(jnp.int32, square, 1), 1.0, 0.0
    ).astype(F32)
    factor_step(table, 0)
    landed(1, 2)
    hop(2, 2)
    multiply(1, everything)
    core_start(1)
    multiply(2, everything)
    core_start(2)
    factor_step(table, 1)
    x_start(1)
    x_start(2)
    landed(2, 0)
    hop(3, 0)
    factor_step(table, 2)
    y_start(1)
    y_start(2)
    factor_step(table, 3)
    landed(2, 1)
    hop(3, 1)
    deliver(1)
    deliver(2)
    factor_step(table, 4)
    landed(2, 2)
    hop(3, 2)
    multiply(3, everything)
    core_start(3)
    multiply(4, everything)
    core_start(4)
    factor_step(table, 5)
    x_start(3)
    x_start(4)
    factor_step(table, 6)
    y_start(3)
    y_start(4)
    factor_step(table, 7)
    deliver(3)
    deliver(4)
    for comp in range(3):
        landed(3, comp)
        multiply(5, (comp,))
        multiply(6, (comp,))
    core_start(5)
    core_start(6)
    x_start(5)
    x_start(6)
    y_start(5)
    y_start(6)
    deliver(5)
    deliver(6)
    for slot in range(7):
        collect(slot)
    out_ref[...] = exact_dot(table[:, S:], fin[1:49], NT)

    @pl.when(s < SPACE - 1)
    def _():
        to_right.wait_send()

    @pl.when(s > 0)
    def _():
        to_left.wait_send()

    for way in range(2):
        arrived(xt.at[0:REACH], z_send.at[way])
    arrived(yr.at[0], g_send.at[0])
    arrived(xr.at[0], g_send.at[1])
    for p in range(LAST + 1):
        if p == LAST:
            pl.when(core == 1)(lambda: core_copy(LAST).wait_send())
        else:
            core_copy(p).wait_send()

        def rest(p=p):
            arrived(xr.at[p], x_send.at[p])
            arrived(yr.at[p], y_send.at[p])

        on_pair(p, rest)
        if p > 0:
            sent(p)


def body(velocity, metric):
    cells, pairs = velocity.shape[1], len(PAIRS)
    dma = pltpu.SemaphoreType.DMA
    return pl.pallas_call(
        kernel,
        out_shape=jax.ShapeDtypeStruct((S, 3072 // SPACE), F32),
        in_specs=[pl.BlockSpec(memory_space=pltpu.VMEM)] * 2,
        out_specs=pl.BlockSpec(memory_space=pltpu.VMEM),
        scratch_shapes=[
            pltpu.VMEM((2 * REACH + 1, 3, S, cells), jnp.bfloat16),
            pltpu.VMEM((2, 3, 16, S), jnp.bfloat16),
            pltpu.VMEM((pairs, 2, S, S), F32),
            pltpu.VMEM((pairs, S, S), F32),
            pltpu.VMEM((pairs, S, S), F32),
            pltpu.VMEM((pairs, X - 1, S // X, S), F32),
            pltpu.VMEM((pairs, S // X, S), F32),
            pltpu.VMEM((pairs, Y - 1, 8, S), F32),
            pltpu.VMEM((pairs, 8, S), F32),
            pltpu.VMEM((S, S), F32),
            pltpu.VMEM((S, 2 * S), F32),
            pltpu.VMEM((56, S), F32),
            dma((2,)), dma((2,)), dma((2,)), dma((2, REACH, 3)),
            dma((pairs,)), dma((pairs,)), dma((pairs,)), dma((pairs,)), dma((pairs,)), dma((pairs,)),
            dma((2,)), dma((2,)), dma((pairs, 2)), dma((7,)),
        ],
        compiler_params=pltpu.CompilerParams(
            collective_id=0, has_side_effects=True, vmem_limit_bytes=48 * 1024 * 1024
        ),
    )(velocity, metric)


def solution(mesh):
    in_specs = (P(None, "space", "tm"), P("space"))
    out_specs = P("tm", "space")
    return jax.shard_map(body, mesh=mesh, in_specs=in_specs, out_specs=out_specs, check_vma=False)
```

time: 413 us -> 108 us (0.26)
  the two profiles are of different devices: /device:TPU:2 before, /device:TPU:105 now
where the time goes in v1:
time: 108 us
  Pallas kernels  105 us (97%)
  local copies, waits for them, and re-layouts  2.44 us (2%)
    pallas_call x1, Pallas kernels, body(): pl.pallas_call(kernel, out_shape=jax.ShapeDtypeStruct((S, 3072 // SPACE),...  105 us

profile of v1, /device:TPU:105, one launch (start us, length us, event | category | flops | bytes accessed | tf_op | source)
XLA Modules:
  0.0 107.8 jit_solution(13205969219251728216)
XLA Ops:
  0.0 0.0 copy-start
  0.0 1.1 copy-done
  1.1 0.0 copy-start.1
  1.1 0.7 copy-done.1
  1.7 105.3 %shard_map.28 = f32[256,48]{1,0:T(8,128)S(1)} custom-call(bf16[3,384,256]{2,1,0:T(8,128)(2,1)S(1)} %copy-done, f32[384]{0:T(512)S(1)} %copy-done.1), custom_call_target="tpu_custom_call" | custom-call | tf_op jit(solution)/shard_map/pallas_call | solution.py:396
  107.1 0.7 copy.3
Async XLA Ops:
  0.0 1.1 copy-start
  1.1 0.7 copy-start.1

commit v2 on v1

v2 whole, which is shorter than its diff:
```python
import jax
import jax.numpy as jnp
from jax import lax
from jax.experimental import pallas as pl
from jax.experimental.pallas import tpu as pltpu
from jax.sharding import PartitionSpec as P

MESH = pl.DeviceIdType.MESH
X, Y, Z = 4, 8, 12
SPACE = 2 * X * Y
S = 256
PAIRS = ((0, 0), (0, 1), (-1, 1), (-1, 2), (-2, 2), (-2, 3), (-3, 3))
LAST = len(PAIRS) - 1
REACH = 3
THIRD = 128
ORDER = (1, 0, 2)
BLOCK = 64
WIDTH = 8
NT = (((1,), (1,)), ((), ()))
NN = (((1,), (0,)), ((), ()))
F32 = jnp.float32


def exact_dot(left, right, dims):
    return lax.dot_general(
        left, right, dims, precision=lax.Precision.HIGHEST, preferred_element_type=F32
    )


def eliminate(work):
    below = lax.broadcasted_iota(jnp.int32, work.shape, 0)
    for first in range(0, BLOCK, WIDTH):
        columns = [jnp.broadcast_to(work[:, k : k + 1], work.shape) for k in range(first, first + WIDTH)]
        rows = [work[k : k + 1, :] for k in range(first, first + WIDTH)]
        scales = []
        for t in range(WIDTH):
            k = first + t
            scale = jnp.where(below > k, columns[t] * (1.0 / columns[t][k : k + 1, :]), 0.0)
            scales.append(scale)
            for u in range(t + 1, WIDTH):
                columns[u] = columns[u] - scale * columns[u][k : k + 1, :]
                rows[u] = rows[u] - scale[first + u : first + u + 1, :] * rows[t]
        for scale, pivot_row in zip(scales, rows):
            work = work - scale * pivot_row
    return work


def factor_step(table, j):
    low = j * BLOCK
    rows = table[low : low + BLOCK, :]
    row_at = lax.broadcasted_iota(jnp.int32, (BLOCK, BLOCK), 0)
    lane_at = lax.broadcasted_iota(jnp.int32, (BLOCK, BLOCK), 1)
    eye = jnp.where(row_at == lane_at, 1.0, 0.0).astype(F32)
    work = eliminate(jnp.concatenate([rows[:, low : low + BLOCK], eye], axis=1))
    pivots = jnp.sum(jnp.where(row_at == lane_at, work[:, :BLOCK], 0.0), axis=1, keepdims=True)
    inverse = work[:, BLOCK:] / jnp.sqrt(pivots)
    solved = exact_dot(inverse, rows, NN)
    table[low : low + BLOCK, :] = solved
    if low + BLOCK < S:
        panel = jnp.transpose(solved[:, :S])[low + BLOCK :, :]
        table[low + BLOCK :, :] = table[low + BLOCK :, :] - exact_dot(panel, solved, NN)


def kernel(
    v_hbm, m_hbm, out_ref,
    v_ref, m_ref, xt, halo, part, cr, cs, xr, xs, yr, ys, last_yr, last_s, last_xr, gram, table, fin,
    in_sem, halo_send, halo_recv, z_send, z_recv, c_send, c_recv, x_send, x_recv, y_send, y_recv,
    g_send, g_recv, f_send, f_recv,
):
    s = lax.axis_index("space")
    c = lax.axis_index("tm")
    core = lax.rem(s, 2)
    x = lax.rem(lax.div(s, 2), X)
    y = lax.div(s, 2 * X)
    plus, minus = lax.rem(c + 1, Z), lax.rem(c + Z - 1, Z)
    right, left = lax.rem(s + 1, SPACE), lax.rem(s + SPACE - 1, SPACE)
    cells = v_ref.shape[1]

    def at(y_at, x_at, core_at):
        return (y_at * X + x_at) * 2 + core_at

    partner = at(y, x, 1 - core)
    x_peers = [at(y, lax.rem(x + t, X), core) for t in range(X)]
    y_peers = [at(lax.rem(y + t, Y), x, core) for t in range(Y)]

    barrier = pltpu.get_barrier_semaphore()
    greeted = [(s, plus), (s, minus), (right, c), (left, c), (partner, c)]
    greeted += [(peer, c) for peer in x_peers[1:] + y_peers[1:]]
    for device in greeted:
        pl.semaphore_signal(barrier, inc=1, device_id=device, device_id_type=MESH)
    fetch_v = pltpu.make_async_copy(v_hbm, v_ref, in_sem.at[0])
    fetch_m = pltpu.make_async_copy(m_hbm, m_ref, in_sem.at[1])
    fetch_v.start()
    fetch_m.start()
    fetch_v.wait()
    fetch_m.wait()
    pl.semaphore_wait(barrier, len(greeted))

    def remote(src, dst, send, recv, device):
        return pltpu.make_async_remote_copy(
            src_ref=src, dst_ref=dst, send_sem=send, recv_sem=recv, device_id=device, device_id_type=MESH
        )

    def arrived(ref, sem):
        pltpu.make_async_copy(ref, ref, sem).wait()

    to_right = remote(v_ref.at[:, cells - 16 :, :], halo.at[0], halo_send.at[0], halo_recv.at[0], (right, c))
    to_left = remote(v_ref.at[:, :16, :], halo.at[1], halo_send.at[1], halo_recv.at[1], (left, c))

    @pl.when(s < SPACE - 1)
    def _():
        to_right.start()

    @pl.when(s > 0)
    def _():
        to_left.start()

    def halo_landed():
        @pl.when(s > 0)
        def _():
            to_right.wait_recv()

        @pl.when(s == 0)
        def _():
            halo[0] = jnp.zeros_like(halo[0])

        @pl.when(s < SPACE - 1)
        def _():
            to_left.wait_recv()

        @pl.when(s == SPACE - 1)
        def _():
            halo[1] = jnp.zeros_like(halo[1])

    row = lax.broadcasted_iota(jnp.int32, (THIRD, S), 0)

    def features(q):
        low = q * THIRD
        start, stop = max(low - 16, 0), min(low + THIRD + 16, cells)
        here = slice(low - start, low - start + THIRD)
        spacing = jnp.transpose(jnp.broadcast_to(m_ref[low : low + THIRD].reshape(1, THIRD), (THIRD, THIRD)))
        spacing = jnp.concatenate([spacing, spacing], axis=1)
        gradients = []
        for k in range(3):
            field = v_ref[k, start:stop].astype(F32)
            after = pltpu.roll(field, stop - start - 1, 0)[here]
            before = pltpu.roll(field, 1, 0)[here]
            if stop == cells:
                edge = jnp.broadcast_to(halo[1, k].astype(F32)[0:1, :], (THIRD, S))
                after = jnp.where(row == THIRD - 1, edge, after)
            if start == 0:
                edge = jnp.broadcast_to(halo[0, k].astype(F32)[15:16, :], (THIRD, S))
                before = jnp.where(row == 0, edge, before)
            gradients.append(spacing * (after - before) * 0.5)
        center = [v_ref[k, low : low + THIRD].astype(F32) for k in range(2)]
        gradients[2] = gradients[2] + center[0] * gradients[1] - center[1] * gradients[0]
        for k in range(3):
            xt[REACH, q, :, k * THIRD : (k + 1) * THIRD] = jnp.transpose(gradients[k]).astype(jnp.bfloat16)

    def hop(t, q):
        for way, device, sign in ((0, plus, -1), (1, minus, 1)):
            remote(
                xt.at[REACH + sign * (t - 1), q], xt.at[REACH + sign * t, q],
                z_send.at[way], z_recv.at[way, t - 1, q], (s, device),
            ).start()

    def landed(t, q):
        for way, sign in ((0, -1), (1, 1)):
            arrived(xt.at[REACH + sign * t, q], z_recv.at[way, t - 1, q])

    def multiply(p, thirds):
        low, high = PAIRS[p]
        for q in thirds:
            lower, upper = xt[REACH + low, q], xt[REACH + high, q]
            for side, (one, other) in enumerate(((upper, lower), (lower, upper))):
                if side == 1 and p in (0, LAST):
                    continue
                term = lax.dot_general(one, other, NT, preferred_element_type=F32)
                if q == ORDER[0]:
                    part[p, side] = term
                else:
                    part[p, side] = part[p, side] + term

    def on_pair(p, body):
        if p == LAST:
            pl.when(core == 0)(body)
        else:
            body()

    def stages(p):
        x_axis = (x, x_peers, X, x_send.at[p], x_recv.at[p])
        y_axis = (y, y_peers, Y, y_send.at[p], y_recv.at[p])
        if p == LAST:
            return (y_axis, last_yr, last_s, S // Y), (x_axis, last_xr, last_s, 8)
        return (x_axis, xr.at[p], xs.at[p], S // X), (y_axis, yr.at[p], xs.at[p], 8)

    def piece(p, t):
        (at_axis, _, count, _, _), _, _, size = stages(p)[0]
        return pl.ds(pl.multiple_of(lax.rem(at_axis + t, count) * size, size), size)

    def core_copy(p, t):
        side = 0 if p in (0, LAST) else 1 - core
        rows = piece(p, t)
        return remote(part.at[p, side, rows], cr.at[p, rows], c_send.at[p], c_recv.at[p, t], (partner, c))

    def core_start(p):
        def body():
            for t in order(p):
                core_copy(p, t).start()

        if p == LAST:
            pl.when(core == 1)(body)
        else:
            body()

    def order(p):
        count = stages(p)[0][0][2]
        return tuple(range(1, count)) + (0,)

    def first_stage(p):
        (_, peers, _, send, recv), landing, _, _ = stages(p)[0]

        def body():
            for t in order(p):
                core_copy(p, t).wait_recv()
                rows = piece(p, t)
                own = part[p, 0, rows] if p in (0, LAST) else part[p, core, rows]
                cs[p, rows] = own + cr[p, rows]
                if t > 0:
                    remote(cs.at[p, rows], landing.at[t - 1], send, recv, (peers[t], c)).start()

        on_pair(p, body)

    def second_stage(p):
        (_, _, count, _, recv), landing, summed, _ = stages(p)[0]
        (at_axis, peers, others, send, recv_next), landing_next, _, size = stages(p)[1]

        def body():
            arrived(landing, recv)
            total = cs[p, piece(p, 0)]
            for t in range(count - 1):
                total = total + landing[t]
            summed[...] = total
            for t in range(1, others):
                chunk = pl.ds(pl.multiple_of(lax.rem(at_axis + t, others) * size, size), size)
                remote(summed.at[chunk], landing_next.at[t - 1], send, recv_next, (peers[t], c)).start()

        on_pair(p, body)

    def finish(p):
        (at_axis, _, count, _, recv), landing, summed, size = stages(p)[1]
        arrived(landing, recv)
        total = summed[pl.ds(pl.multiple_of(at_axis * size, size), size)]
        for t in range(count - 1):
            total = total + landing[t]
        return total

    def gram_y():
        rows = pl.ds(pl.multiple_of(x * 64 + y * 8, 8), 8)
        gram[rows] = finish(0)
        for t in range(1, Y):
            remote(gram.at[rows], gram.at[rows], g_send.at[0], g_recv.at[0], (y_peers[t], c)).start()

    def gram_x():
        arrived(yr.at[0], g_recv.at[0])
        rows = pl.ds(pl.multiple_of(x * 64, 64), 64)
        for t in range(1, X):
            remote(gram.at[rows], gram.at[rows], g_send.at[1], g_recv.at[1], (x_peers[t], c)).start()

    def gram_finish():
        arrived(xr.at[0], g_recv.at[1])
        table[:, :S] = gram[...]
        square = (S, S)
        table[:, S:] = jnp.where(
            lax.broadcasted_iota(jnp.int32, square, 0) == lax.broadcasted_iota(jnp.int32, square, 1), 1.0, 0.0
        ).astype(F32)

    def place(p):
        low, high = PAIRS[p]
        unit = y * X + x if p == LAST else x * Y + y
        lanes_of = jnp.where(core == 0, low, high)
        rows_of = jnp.where(core == 0, high, low)
        group = lax.rem(c + lanes_of + Z, Z)
        number = lax.rem(c + rows_of + Z, Z) * 32 + unit
        owner, slot = lax.div(number, 6), lax.rem(number, 6)
        return group, owner, slot

    def to_owner(p):
        group, owner, slot = place(p)
        rows = pl.ds(pl.multiple_of(slot * 8, 8), 8)
        mine = jnp.logical_and(owner == s, group == c)
        return mine, rows, remote(ys.at[p], fin.at[rows], f_send.at[p, 0], f_recv.at[slot], (owner, group))

    def to_ahead(p):
        group, owner, slot = place(p)
        ahead = lax.rem(owner + SPACE - 1, SPACE)
        mine = jnp.logical_and(ahead == s, group == c)
        return slot == 0, mine, remote(ys.at[p], fin.at[48:56], f_send.at[p, 1], f_recv.at[6], (ahead, group))

    def deliver(p):
        def body():
            ys[p] = finish(p)
            mine, rows, copy = to_owner(p)

            @pl.when(mine)
            def _():
                fin[rows] = ys[p]

            @pl.when(jnp.logical_not(mine))
            def _():
                copy.start()

            first, mine_ahead, copy_ahead = to_ahead(p)

            @pl.when(jnp.logical_and(first, mine_ahead))
            def _():
                fin[48:56] = ys[p]

            @pl.when(jnp.logical_and(first, jnp.logical_not(mine_ahead)))
            def _():
                copy_ahead.start()

        on_pair(p, body)

    def sent(p):
        def body():
            mine, _, copy = to_owner(p)

            @pl.when(jnp.logical_not(mine))
            def _():
                copy.wait_send()

            first, mine_ahead, copy_ahead = to_ahead(p)

            @pl.when(jnp.logical_and(first, jnp.logical_not(mine_ahead)))
            def _():
                copy_ahead.wait_send()

        on_pair(p, body)

    def collect(slot):
        number = lax.rem(s * 6 + slot, SPACE * 6)
        apart = lax.rem(lax.div(number, 32) - c + Z, Z)
        within = lax.rem(number, 32)
        near = apart <= Z // 2
        home = jnp.where(near, lax.div(apart, 2), Z - lax.div(Z - apart + 1, 2))
        y_at = jnp.where(apart == Z // 2, lax.div(within, X), lax.rem(within, Y))
        x_at = jnp.where(apart == Z // 2, lax.rem(within, X), lax.div(within, Y))
        source = at(y_at, x_at, jnp.where(near, 0, 1))
        own = jnp.logical_and(source == s, lax.rem(home, Z) == 0)
        rows = slice(slot * 8, slot * 8 + 8)

        @pl.when(apart == 0)
        def _():
            fin[rows] = gram[pl.ds(pl.multiple_of(within * 8, 8), 8)]

        @pl.when(jnp.logical_and(apart != 0, jnp.logical_not(own)))
        def _():
            arrived(fin.at[rows], f_recv.at[slot])

    one, two, three = ORDER
    features(one)
    hop(1, one)
    halo_landed()
    features(two)
    hop(1, two)
    features(three)
    hop(1, three)
    multiply(0, ORDER)
    core_start(0)
    landed(1, one)
    hop(2, one)
    first_stage(0)
    landed(1, two)
    hop(2, two)
    second_stage(0)
    landed(1, three)
    hop(2, three)
    gram_y()
    for p in (1, 2):
        multiply(p, ORDER)
        core_start(p)
    landed(2, one)
    hop(3, one)
    gram_x()
    first_stage(1)
    first_stage(2)
    landed(2, two)
    hop(3, two)
    gram_finish()
    factor_step(table, 0)
    second_stage(1)
    second_stage(2)
    landed(2, three)
    hop(3, three)
    for p in (3, 4):
        multiply(p, ORDER)
        core_start(p)
    factor_step(table, 1)
    deliver(1)
    deliver(2)
    landed(3, one)
    multiply(5, (one,))
    multiply(6, (one,))
    first_stage(3)
    first_stage(4)
    factor_step(table, 2)
    landed(3, two)
    multiply(5, (two,))
    multiply(6, (two,))
    second_stage(3)
    second_stage(4)
    landed(3, three)
    multiply(5, (three,))
    core_start(5)
    multiply(6, (three,))
    core_start(6)
    factor_step(table, 3)
    first_stage(5)
    first_stage(6)
    deliver(3)
    deliver(4)
    second_stage(5)
    second_stage(6)
    deliver(5)
    deliver(6)
    for slot in range(7):
        collect(slot)
    out_ref[...] = exact_dot(fin[1:49], table[:, S:], NT)

    @pl.when(s < SPACE - 1)
    def _():
        to_right.wait_send()

    @pl.when(s > 0)
    def _():
        to_left.wait_send()

    for way in range(2):
        arrived(xt.at[0:REACH], z_send.at[way])
    arrived(yr.at[0], g_send.at[0])
    arrived(xr.at[0], g_send.at[1])
    for p in range(LAST + 1):
        if p == LAST:
            pl.when(core == 1)(lambda: arrived(cr.at[LAST], c_send.at[LAST]))
        else:
            arrived(cr.at[p], c_send.at[p])

        def rest(p=p):
            for (_, _, _, send, _), landing, _, _ in stages(p):
                arrived(landing, send)

        on_pair(p, rest)
        if p > 0:
            sent(p)


def body(velocity, metric):
    cells, pairs = velocity.shape[1], len(PAIRS)
    dma = pltpu.SemaphoreType.DMA
    tiles = pl.pallas_call(
        kernel,
        out_shape=jax.ShapeDtypeStruct((3072 // SPACE, S), F32),
        in_specs=[pl.BlockSpec(memory_space=pl.ANY)] * 2,
        out_specs=pl.BlockSpec(memory_space=pltpu.VMEM),
        scratch_shapes=[
            pltpu.VMEM((3, cells, S), jnp.bfloat16),
            pltpu.VMEM((cells,), F32),
            pltpu.VMEM((2 * REACH + 1, 3, S, cells), jnp.bfloat16),
            pltpu.VMEM((2, 3, 16, S), jnp.bfloat16),
            pltpu.VMEM((pairs, 2, S, S), F32),
            pltpu.VMEM((pairs, S, S), F32),
            pltpu.VMEM((pairs, S, S), F32),
            pltpu.VMEM((pairs - 1, X - 1, S // X, S), F32),
            pltpu.VMEM((pairs - 1, S // X, S), F32),
            pltpu.VMEM((pairs - 1, Y - 1, 8, S), F32),
            pltpu.VMEM((pairs, 8, S), F32),
            pltpu.VMEM((Y - 1, S // Y, S), F32),
            pltpu.VMEM((S // Y, S), F32),
            pltpu.VMEM((X - 1, 8, S), F32),
            pltpu.VMEM((S, S), F32),
            pltpu.VMEM((S, 2 * S), F32),
            pltpu.VMEM((56, S), F32),
            dma((2,)), dma((2,)), dma((2,)), dma((2,)), dma((2, REACH, 3)),
            dma((pairs,)), dma((pairs, Y)), dma((pairs,)), dma((pairs,)), dma((pairs,)), dma((pairs,)),
            dma((2,)), dma((2,)), dma((pairs, 2)), dma((7,)),
        ],
        compiler_params=pltpu.CompilerParams(
            collective_id=0, has_side_effects=True, vmem_limit_bytes=56 * 1024 * 1024
        ),
    )(velocity, metric)
    return tiles.T


def solution(mesh):
    in_specs = (P(None, "space", "tm"), P("space"))
    out_specs = P("tm", "space")
    return jax.shard_map(body, mesh=mesh, in_specs=in_specs, out_specs=out_specs, check_vma=False)
```

time: 108 us -> 79.3 us (0.73)
  the two profiles are of different devices: /device:TPU:105 before, /device:TPU:4 now
where the time goes in v2:
time: 79.3 us; the launch traced here: 79.1 us
  Pallas kernels  77.7 us (98%)
  local copies, waits for them, and re-layouts  1.42 us (2%)
    pallas_call x1, Pallas kernels, body(): pl.pallas_call(kernel, out_shape=jax.ShapeDtypeStruct((3072 // SPACE, S),...  77.7 us

profile of v2, /device:TPU:4, one launch (start us, length us, event | category | flops | bytes accessed | tf_op | source)
XLA Modules:
  0.0 79.1 jit_solution(14244315044347289805)
XLA Ops:
  0.0 77.7 %shard_map.28 = f32[48,256]{1,0:T(8,128)} custom-call(bf16[3,384,256]{2,1,0:T(8,128)(2,1)} %v_hbm.1, f32[384]{0:T(512)} %m_hbm.1), custom_call_target="tpu_custom_call" | custom-call | tf_op jit(solution)/shard_map/pallas_call | solution.py:461
  77.7 1.4 %copy.4 = f32[256,48]{0,1:T(8,128)} copy(f32[256,48]{0,1:T(8,128)} %bitcast.1) | data formatting | bytes 98304

commit v3 on v2

--- a/solution.py
+++ b/solution.py
@@ -13,6 +13,7 @@
 LAST = len(PAIRS) - 1
 REACH = 3
 THIRD = 128
+HALF = S // 2
 ORDER = (1, 0, 2)
 BLOCK = 64
 WIDTH = 8
@@ -63,7 +64,8 @@
 
 def kernel(
     v_hbm, m_hbm, out_ref,
-    v_ref, m_ref, xt, halo, part, cr, cs, xr, xs, yr, ys, last_yr, last_s, last_xr, gram, table, fin,
+    v_ref, m_ref, xt, halo, part, cr, cs, xr, xs, yr, ys,
+    last_part, last_cr, last_cs, last_yr, last_s, last_xr, last_ys, gram, table, fin,
     in_sem, halo_send, halo_recv, z_send, z_recv, c_send, c_recv, x_send, x_recv, y_send, y_recv,
     g_send, g_recv, f_send, f_recv,
 ):
@@ -94,7 +96,6 @@
     fetch_m.start()
     fetch_v.wait()
     fetch_m.wait()
-    pl.semaphore_wait(barrier, len(greeted))
 
     def remote(src, dst, send, recv, device):
         return pltpu.make_async_remote_copy(
@@ -107,13 +108,16 @@
     to_right = remote(v_ref.at[:, cells - 16 :, :], halo.at[0], halo_send.at[0], halo_recv.at[0], (right, c))
     to_left = remote(v_ref.at[:, :16, :], halo.at[1], halo_send.at[1], halo_recv.at[1], (left, c))
 
-    @pl.when(s < SPACE - 1)
-    def _():
-        to_right.start()
-
-    @pl.when(s > 0)
-    def _():
-        to_left.start()
+    def enter():
+        pl.semaphore_wait(barrier, len(greeted))
+
+        @pl.when(s < SPACE - 1)
+        def _():
+            to_right.start()
+
+        @pl.when(s > 0)
+        def _():
+            to_left.start()
 
     def halo_landed():
         @pl.when(s > 0)
@@ -168,24 +172,21 @@
         for way, sign in ((0, -1), (1, 1)):
             arrived(xt.at[REACH + sign * t, q], z_recv.at[way, t - 1, q])
 
+    def gather(ref, at_index, term, q):
+        ref[at_index] = term if q == ORDER[0] else ref[at_index] + term
+
     def multiply(p, thirds):
         low, high = PAIRS[p]
         for q in thirds:
             lower, upper = xt[REACH + low, q], xt[REACH + high, q]
-            for side, (one, other) in enumerate(((upper, lower), (lower, upper))):
-                if side == 1 and p in (0, LAST):
-                    continue
-                term = lax.dot_general(one, other, NT, preferred_element_type=F32)
-                if q == ORDER[0]:
-                    part[p, side] = term
-                else:
-                    part[p, side] = part[p, side] + term
-
-    def on_pair(p, body):
-        if p == LAST:
-            pl.when(core == 0)(body)
-        else:
-            body()
+            term = lax.dot_general(upper, lower, NT, preferred_element_type=F32)
+            if p == LAST:
+                gather(last_part, 0, term[:, :HALF], q)
+                gather(last_part, 1, term[:, HALF:], q)
+                continue
+            gather(part, (p, 0), term, q)
+            if p > 0:
+                gather(part, (p, 1), lax.dot_general(lower, upper, NT, preferred_element_type=F32), q)
 
     def stages(p):
         x_axis = (x, x_peers, X, x_send.at[p], x_recv.at[p])
@@ -194,58 +195,51 @@
             return (y_axis, last_yr, last_s, S // Y), (x_axis, last_xr, last_s, 8)
         return (x_axis, xr.at[p], xs.at[p], S // X), (y_axis, yr.at[p], xs.at[p], 8)
 
+    def core_refs(p):
+        if p == LAST:
+            return last_part.at[core], last_part.at[1 - core], last_cr, last_cs
+        if p == 0:
+            return part.at[0, 0], part.at[0, 0], cr.at[0], cs.at[0]
+        return part.at[p, core], part.at[p, 1 - core], cr.at[p], cs.at[p]
+
     def piece(p, t):
         (at_axis, _, count, _, _), _, _, size = stages(p)[0]
         return pl.ds(pl.multiple_of(lax.rem(at_axis + t, count) * size, size), size)
 
-    def core_copy(p, t):
-        side = 0 if p in (0, LAST) else 1 - core
-        rows = piece(p, t)
-        return remote(part.at[p, side, rows], cr.at[p, rows], c_send.at[p], c_recv.at[p, t], (partner, c))
-
-    def core_start(p):
-        def body():
-            for t in order(p):
-                core_copy(p, t).start()
-
-        if p == LAST:
-            pl.when(core == 1)(body)
-        else:
-            body()
-
     def order(p):
         count = stages(p)[0][0][2]
         return tuple(range(1, count)) + (0,)
 
+    def core_copy(p, t):
+        _, given, landing, _ = core_refs(p)
+        rows = piece(p, t)
+        return remote(given.at[rows], landing.at[rows], c_send.at[p], c_recv.at[p, t], (partner, c))
+
+    def core_start(p):
+        for t in order(p):
+            core_copy(p, t).start()
+
     def first_stage(p):
         (_, peers, _, send, recv), landing, _, _ = stages(p)[0]
-
-        def body():
-            for t in order(p):
-                core_copy(p, t).wait_recv()
-                rows = piece(p, t)
-                own = part[p, 0, rows] if p in (0, LAST) else part[p, core, rows]
-                cs[p, rows] = own + cr[p, rows]
-                if t > 0:
-                    remote(cs.at[p, rows], landing.at[t - 1], send, recv, (peers[t], c)).start()
-
-        on_pair(p, body)
+        kept, _, received, summed = core_refs(p)
+        for t in order(p):
+            core_copy(p, t).wait_recv()
+            rows = piece(p, t)
+            summed[rows] = kept[rows] + received[rows]
+            if t > 0:
+                remote(summed.at[rows], landing.at[t - 1], send, recv, (peers[t], c)).start()
 
     def second_stage(p):
         (_, _, count, _, recv), landing, summed, _ = stages(p)[0]
         (at_axis, peers, others, send, recv_next), landing_next, _, size = stages(p)[1]
-
-        def body():
-            arrived(landing, recv)
-            total = cs[p, piece(p, 0)]
-            for t in range(count - 1):
-                total = total + landing[t]
-            summed[...] = total
-            for t in range(1, others):
-                chunk = pl.ds(pl.multiple_of(lax.rem(at_axis + t, others) * size, size), size)
-                remote(summed.at[chunk], landing_next.at[t - 1], send, recv_next, (peers[t], c)).start()
-
-        on_pair(p, body)
+        arrived(landing, recv)
+        total = core_refs(p)[3][piece(p, 0)]
+        for t in range(count - 1):
+            total = total + landing[t]
+        summed[...] = total
+        for t in range(1, others):
+            chunk = pl.ds(pl.multiple_of(lax.rem(at_axis + t, others) * size, size), size)
+            remote(summed.at[chunk], landing_next.at[t - 1], send, recv_next, (peers[t], c)).start()
 
     def finish(p):
         (at_axis, _, count, _, recv), landing, summed, size = stages(p)[1]
@@ -275,68 +269,74 @@
             lax.broadcasted_iota(jnp.int32, square, 0) == lax.broadcasted_iota(jnp.int32, square, 1), 1.0, 0.0
         ).astype(F32)
 
+    def unit_of(p):
+        return (last_ys, pl.ds(pl.multiple_of(core * HALF, HALF), HALF)) if p == LAST else (ys.at[p], slice(None))
+
     def place(p):
         low, high = PAIRS[p]
-        unit = y * X + x if p == LAST else x * Y + y
-        lanes_of = jnp.where(core == 0, low, high)
-        rows_of = jnp.where(core == 0, high, low)
+        if p == LAST:
+            unit, lanes_of, rows_of, lane_sem = y * X + x, low, high, core
+        else:
+            unit, lane_sem = x * Y + y, 0
+            lanes_of = jnp.where(core == 0, low, high)
+            rows_of = jnp.where(core == 0, high, low)
         group = lax.rem(c + lanes_of + Z, Z)
         number = lax.rem(c + rows_of + Z, Z) * 32 + unit
         owner, slot = lax.div(number, 6), lax.rem(number, 6)
-        return group, owner, slot
+        return group, owner, slot, lane_sem
 
     def to_owner(p):
-        group, owner, slot = place(p)
+        group, owner, slot, lane_sem = place(p)
+        unit, lanes = unit_of(p)
         rows = pl.ds(pl.multiple_of(slot * 8, 8), 8)
         mine = jnp.logical_and(owner == s, group == c)
-        return mine, rows, remote(ys.at[p], fin.at[rows], f_send.at[p, 0], f_recv.at[slot], (owner, group))
+        copy = remote(unit, fin.at[rows, lanes], f_send.at[p, 0], f_recv.at[slot, lane_sem], (owner, group))
+        return mine, rows, copy
 
     def to_ahead(p):
-        group, owner, slot = place(p)
+        group, owner, slot, lane_sem = place(p)
+        unit, lanes = unit_of(p)
         ahead = lax.rem(owner + SPACE - 1, SPACE)
         mine = jnp.logical_and(ahead == s, group == c)
-        return slot == 0, mine, remote(ys.at[p], fin.at[48:56], f_send.at[p, 1], f_recv.at[6], (ahead, group))
+        copy = remote(unit, fin.at[48:56, lanes], f_send.at[p, 1], f_recv.at[6, lane_sem], (ahead, group))
+        return slot == 0, mine, copy
 
     def deliver(p):
-        def body():
-            ys[p] = finish(p)
-            mine, rows, copy = to_owner(p)
+        unit, _ = unit_of(p)
+        unit[...] = finish(p)
+        mine, rows, copy = to_owner(p)
+        first, mine_ahead, copy_ahead = to_ahead(p)
+
+        @pl.when(jnp.logical_not(mine))
+        def _():
+            copy.start()
+
+        @pl.when(jnp.logical_and(first, jnp.logical_not(mine_ahead)))
+        def _():
+            copy_ahead.start()
+
+        if p == 1:
 
             @pl.when(mine)
             def _():
-                fin[rows] = ys[p]
-
-            @pl.when(jnp.logical_not(mine))
-            def _():
-                copy.start()
-
-            first, mine_ahead, copy_ahead = to_ahead(p)
+                fin[rows] = unit[...]
 
             @pl.when(jnp.logical_and(first, mine_ahead))
             def _():
-                fin[48:56] = ys[p]
-
-            @pl.when(jnp.logical_and(first, jnp.logical_not(mine_ahead)))
-            def _():
-                copy_ahead.start()
-
-        on_pair(p, body)
+                fin[48:56] = unit[...]
 
     def sent(p):
-        def body():
-            mine, _, copy = to_owner(p)
-
-            @pl.when(jnp.logical_not(mine))
-            def _():
-                copy.wait_send()
-
-            first, mine_ahead, copy_ahead = to_ahead(p)
-
-            @pl.when(jnp.logical_and(first, jnp.logical_not(mine_ahead)))
-            def _():
-                copy_ahead.wait_send()
-
-        on_pair(p, body)
+        mine, _, copy = to_owner(p)
+
+        @pl.when(jnp.logical_not(mine))
+        def _():
+            copy.wait_send()
+
+        first, mine_ahead, copy_ahead = to_ahead(p)
+
+        @pl.when(jnp.logical_and(first, jnp.logical_not(mine_ahead)))
+        def _():
+            copy_ahead.wait_send()
 
     def collect(slot):
         number = lax.rem(s * 6 + slot, SPACE * 6)
@@ -344,9 +344,7 @@
         within = lax.rem(number, 32)
         near = apart <= Z // 2
         home = jnp.where(near, lax.div(apart, 2), Z - lax.div(Z - apart + 1, 2))
-        y_at = jnp.where(apart == Z // 2, lax.div(within, X), lax.rem(within, Y))
-        x_at = jnp.where(apart == Z // 2, lax.rem(within, X), lax.div(within, Y))
-        source = at(y_at, x_at, jnp.where(near, 0, 1))
+        source = at(lax.rem(within, Y), lax.div(within, Y), jnp.where(near, 0, 1))
         own = jnp.logical_and(source == s, lax.rem(home, Z) == 0)
         rows = slice(slot * 8, slot * 8 + 8)
 
@@ -354,12 +352,20 @@
         def _():
             fin[rows] = gram[pl.ds(pl.multiple_of(within * 8, 8), 8)]
 
-        @pl.when(jnp.logical_and(apart != 0, jnp.logical_not(own)))
-        def _():
-            arrived(fin.at[rows], f_recv.at[slot])
+        @pl.when(apart == Z // 2)
+        def _():
+            arrived(fin.at[rows, :HALF], f_recv.at[slot, 0])
+            arrived(fin.at[rows, HALF:], f_recv.at[slot, 1])
+
+        whole = jnp.logical_and(apart != 0, apart != Z // 2)
+
+        @pl.when(jnp.logical_and(whole, jnp.logical_not(own)))
+        def _():
+            arrived(fin.at[rows], f_recv.at[slot, 0])
 
     one, two, three = ORDER
     features(one)
+    enter()
     hop(1, one)
     halo_landed()
     features(two)
@@ -368,65 +374,64 @@
     hop(1, three)
     multiply(0, ORDER)
     core_start(0)
+    first_stage(0)
     landed(1, one)
     hop(2, one)
-    first_stage(0)
+    second_stage(0)
     landed(1, two)
     hop(2, two)
-    second_stage(0)
+    gram_y()
     landed(1, three)
     hop(2, three)
-    gram_y()
-    for p in (1, 2):
-        multiply(p, ORDER)
-        core_start(p)
+    gram_x()
+    multiply(1, ORDER)
+    core_start(1)
+    multiply(2, ORDER)
+    core_start(2)
     landed(2, one)
     hop(3, one)
-    gram_x()
+    gram_finish()
     first_stage(1)
-    first_stage(2)
+    factor_step(table, 0)
     landed(2, two)
     hop(3, two)
-    gram_finish()
-    factor_step(table, 0)
+    first_stage(2)
+    factor_step(table, 1)
+    landed(2, three)
+    hop(3, three)
+    multiply(3, ORDER)
+    core_start(3)
+    multiply(4, ORDER)
+    core_start(4)
     second_stage(1)
     second_stage(2)
-    landed(2, three)
-    hop(3, three)
-    for p in (3, 4):
-        multiply(p, ORDER)
-        core_start(p)
-    factor_step(table, 1)
-    deliver(1)
-    deliver(2)
+    factor_step(table, 2)
     landed(3, one)
     multiply(5, (one,))
     multiply(6, (one,))
     first_stage(3)
-    first_stage(4)
-    factor_step(table, 2)
+    factor_step(table, 3)
+    deliver(1)
+    deliver(2)
     landed(3, two)
     multiply(5, (two,))
     multiply(6, (two,))
-    second_stage(3)
-    second_stage(4)
+    first_stage(4)
     landed(3, three)
     multiply(5, (three,))
     core_start(5)
     multiply(6, (three,))
     core_start(6)
-    factor_step(table, 3)
+    second_stage(3)
+    second_stage(4)
     first_stage(5)
     first_stage(6)
+    second_stage(5)
+    second_stage(6)
     deliver(3)
     deliver(4)
-    second_stage(5)
-    second_stage(6)
     deliver(5)
     deliver(6)
-    for slot in range(7):
-        collect(slot)
-    out_ref[...] = exact_dot(fin[1:49], table[:, S:], NT)
 
     @pl.when(s < SPACE - 1)
     def _():
@@ -441,18 +446,15 @@
     arrived(yr.at[0], g_send.at[0])
     arrived(xr.at[0], g_send.at[1])
     for p in range(LAST + 1):
-        if p == LAST:
-            pl.when(core == 1)(lambda: arrived(cr.at[LAST], c_send.at[LAST]))
-        else:
-            arrived(cr.at[p], c_send.at[p])
-
-        def rest(p=p):
-            for (_, _, _, send, _), landing, _, _ in stages(p):
-                arrived(landing, send)
-
-        on_pair(p, rest)
+        arrived(core_refs(p)[2], c_send.at[p])
+        for (_, _, _, send, _), landing, _, _ in stages(p):
+            arrived(landing, send)
         if p > 0:
             sent(p)
+
+    for slot in range(7):
+        collect(slot)
+    out_ref[...] = exact_dot(fin[1:49], table[:, S:], NT)
 
 
 def body(velocity, metric):
@@ -468,22 +470,26 @@
             pltpu.VMEM((cells,), F32),
             pltpu.VMEM((2 * REACH + 1, 3, S, cells), jnp.bfloat16),
             pltpu.VMEM((2, 3, 16, S), jnp.bfloat16),
-            pltpu.VMEM((pairs, 2, S, S), F32),
-            pltpu.VMEM((pairs, S, S), F32),
-            pltpu.VMEM((pairs, S, S), F32),
+            pltpu.VMEM((pairs - 1, 2, S, S), F32),
+            pltpu.VMEM((pairs - 1, S, S), F32),
+            pltpu.VMEM((pairs - 1, S, S), F32),
             pltpu.VMEM((pairs - 1, X - 1, S // X, S), F32),
             pltpu.VMEM((pairs - 1, S // X, S), F32),
             pltpu.VMEM((pairs - 1, Y - 1, 8, S), F32),
-            pltpu.VMEM((pairs, 8, S), F32),
-            pltpu.VMEM((Y - 1, S // Y, S), F32),
-            pltpu.VMEM((S // Y, S), F32),
-            pltpu.VMEM((X - 1, 8, S), F32),
+            pltpu.VMEM((pairs - 1, 8, S), F32),
+            pltpu.VMEM((2, S, HALF), F32),
+            pltpu.VMEM((S, HALF), F32),
+            pltpu.VMEM((S, HALF), F32),
+            pltpu.VMEM((Y - 1, S // Y, HALF), F32),
+            pltpu.VMEM((S // Y, HALF), F32),
+            pltpu.VMEM((X - 1, 8, HALF), F32),
+            pltpu.VMEM((8, HALF), F32),
             pltpu.VMEM((S, S), F32),
             pltpu.VMEM((S, 2 * S), F32),
             pltpu.VMEM((56, S), F32),
             dma((2,)), dma((2,)), dma((2,)), dma((2,)), dma((2, REACH, 3)),
             dma((pairs,)), dma((pairs, Y)), dma((pairs,)), dma((pairs,)), dma((pairs,)), dma((pairs,)),
-            dma((2,)), dma((2,)), dma((pairs, 2)), dma((7,)),
+            dma((2,)), dma((2,)), dma((pairs, 2)), dma((7, 2)),
         ],
         compiler_params=pltpu.CompilerParams(
             collective_id=0, has_side_effects=True, vmem_limit_bytes=56 * 1024 * 1024

time: 79.3 us -> 75.7 us (0.955)
  the two profiles are of different devices: /device:TPU:4 before, /device:TPU:41 now
where the time goes in v3:
time: 75.7 us; the launch traced here: 75.5 us
  Pallas kernels  74.1 us (98%)
  local copies, waits for them, and re-layouts  1.42 us (2%)
    pallas_call x1, Pallas kernels, body(): pl.pallas_call(kernel, out_shape=jax.ShapeDtypeStruct((3072 // SPACE, S),...  74.1 us

profile of v3, /device:TPU:41, one launch (start us, length us, event | category | flops | bytes accessed | tf_op | source)
XLA Modules:
  0.0 75.5 jit_solution(8488487291370437086)
XLA Ops:
  0.0 74.1 %shard_map.28 = f32[48,256]{1,0:T(8,128)} custom-call(bf16[3,384,256]{2,1,0:T(8,128)(2,1)} %v_hbm.1, f32[384]{0:T(512)} %m_hbm.1), custom_call_target="tpu_custom_call" | custom-call | tf_op jit(solution)/shard_map/pallas_call | solution.py:463
  74.1 1.4 %copy.4 = f32[256,48]{0,1:T(8,128)} copy(f32[256,48]{0,1:T(8,128)} %bitcast.1) | data formatting | bytes 98304

commit v4 on v3

--- a/solution.py
+++ b/solution.py
@@ -90,11 +90,15 @@
     greeted += [(peer, c) for peer in x_peers[1:] + y_peers[1:]]
     for device in greeted:
         pl.semaphore_signal(barrier, inc=1, device_id=device, device_id_type=MESH)
-    fetch_v = pltpu.make_async_copy(v_hbm, v_ref, in_sem.at[0])
-    fetch_m = pltpu.make_async_copy(m_hbm, m_ref, in_sem.at[1])
-    fetch_v.start()
-    fetch_m.start()
-    fetch_v.wait()
+    cuts = (0, THIRD - 16, 2 * THIRD + 16, cells)
+    fetches = [
+        pltpu.make_async_copy(v_hbm.at[:, low:high, :], v_ref.at[:, low:high, :], in_sem.at[i])
+        for i, (low, high) in enumerate(zip(cuts, cuts[1:]))
+    ]
+    fetch_m = pltpu.make_async_copy(m_hbm, m_ref, in_sem.at[3])
+    for fetch in (fetches[1], fetch_m, fetches[0], fetches[2]):
+        fetch.start()
+    fetches[1].wait()
     fetch_m.wait()
 
     def remote(src, dst, send, recv, device):
@@ -108,8 +112,9 @@
     to_right = remote(v_ref.at[:, cells - 16 :, :], halo.at[0], halo_send.at[0], halo_recv.at[0], (right, c))
     to_left = remote(v_ref.at[:, :16, :], halo.at[1], halo_send.at[1], halo_recv.at[1], (left, c))
 
-    def enter():
-        pl.semaphore_wait(barrier, len(greeted))
+    def halo_start():
+        fetches[0].wait()
+        fetches[2].wait()
 
         @pl.when(s < SPACE - 1)
         def _():
@@ -206,9 +211,11 @@
         (at_axis, _, count, _, _), _, _, size = stages(p)[0]
         return pl.ds(pl.multiple_of(lax.rem(at_axis + t, count) * size, size), size)
 
+    def farthest_first(count):
+        return list(range(1, count))
+
     def order(p):
-        count = stages(p)[0][0][2]
-        return tuple(range(1, count)) + (0,)
+        return farthest_first(stages(p)[0][0][2]) + [0]
 
     def core_copy(p, t):
         _, given, landing, _ = core_refs(p)
@@ -237,7 +244,7 @@
         for t in range(count - 1):
             total = total + landing[t]
         summed[...] = total
-        for t in range(1, others):
+        for t in farthest_first(others):
             chunk = pl.ds(pl.multiple_of(lax.rem(at_axis + t, others) * size, size), size)
             remote(summed.at[chunk], landing_next.at[t - 1], send, recv_next, (peers[t], c)).start()
 
@@ -285,8 +292,10 @@
         owner, slot = lax.div(number, 6), lax.rem(number, 6)
         return group, owner, slot, lane_sem
 
+    places = {p: place(p) for p in range(1, LAST + 1)}
+
     def to_owner(p):
-        group, owner, slot, lane_sem = place(p)
+        group, owner, slot, lane_sem = places[p]
         unit, lanes = unit_of(p)
         rows = pl.ds(pl.multiple_of(slot * 8, 8), 8)
         mine = jnp.logical_and(owner == s, group == c)
@@ -294,7 +303,7 @@
         return mine, rows, copy
 
     def to_ahead(p):
-        group, owner, slot, lane_sem = place(p)
+        group, owner, slot, lane_sem = places[p]
         unit, lanes = unit_of(p)
         ahead = lax.rem(owner + SPACE - 1, SPACE)
         mine = jnp.logical_and(ahead == s, group == c)
@@ -338,7 +347,7 @@
         def _():
             copy_ahead.wait_send()
 
-    def collect(slot):
+    def origin(slot):
         number = lax.rem(s * 6 + slot, SPACE * 6)
         apart = lax.rem(lax.div(number, 32) - c + Z, Z)
         within = lax.rem(number, 32)
@@ -346,6 +355,12 @@
         home = jnp.where(near, lax.div(apart, 2), Z - lax.div(Z - apart + 1, 2))
         source = at(lax.rem(within, Y), lax.div(within, Y), jnp.where(near, 0, 1))
         own = jnp.logical_and(source == s, lax.rem(home, Z) == 0)
+        return apart, within, own
+
+    origins = [origin(slot) for slot in range(7)]
+
+    def collect(slot):
+        apart, within, own = origins[slot]
         rows = slice(slot * 8, slot * 8 + 8)
 
         @pl.when(apart == 0)
@@ -365,8 +380,9 @@
 
     one, two, three = ORDER
     features(one)
-    enter()
+    pl.semaphore_wait(barrier, len(greeted))
     hop(1, one)
+    halo_start()
     halo_landed()
     features(two)
     hop(1, two)
@@ -487,7 +503,7 @@
             pltpu.VMEM((S, S), F32),
             pltpu.VMEM((S, 2 * S), F32),
             pltpu.VMEM((56, S), F32),
-            dma((2,)), dma((2,)), dma((2,)), dma((2,)), dma((2, REACH, 3)),
+            dma((4,)), dma((2,)), dma((2,)), dma((2,)), dma((2, REACH, 3)),
             dma((pairs,)), dma((pairs, Y)), dma((pairs,)), dma((pairs,)), dma((pairs,)), dma((pairs,)),
             dma((2,)), dma((2,)), dma((pairs, 2)), dma((7, 2)),
         ],

time: 75.7 us -> 75.6 us (level)
  no operation moved by 1% of the time
where the time goes in v4:
time: 75.6 us; the launch traced here: 75.4 us
  Pallas kernels  74 us (98%)
  local copies, waits for them, and re-layouts  1.42 us (2%)
    pallas_call x1, Pallas kernels, body(): pl.pallas_call(kernel, out_shape=jax.ShapeDtypeStruct((3072 // SPACE, S),...  74 us

profile of v4, /device:TPU:41, one launch (start us, length us, event | category | flops | bytes accessed | tf_op | source)
XLA Modules:
  0.0 75.4 jit_solution(17397453196501064896)
XLA Ops:
  0.0 74.0 %shard_map.28 = f32[48,256]{1,0:T(8,128)} custom-call(bf16[3,384,256]{2,1,0:T(8,128)(2,1)} %v_hbm.1, f32[384]{0:T(512)} %m_hbm.1), custom_call_target="tpu_custom_call" | custom-call | tf_op jit(solution)/shard_map/pallas_call | solution.py:479
  74.0 1.4 %copy.4 = f32[256,48]{0,1:T(8,128)} copy(f32[256,48]{0,1:T(8,128)} %bitcast.1) | data formatting | bytes 98304
